TPU v7x, 32 devices: a whole 2x2x4 slice. The times are simulated.
32 devices in a mesh: dp: 16 (over z, y, core), rows: 2 (over x).
Axes of the slice: x: 2, y: 2, z: 4, core: 2. Of those that a mesh axis runs over, the one named last changes fastest.
Arguments:
- latents: bfloat16 [16, 4, 128, 320], P('dp', 'rows'), may hold values from -6 to 6
- mean_one: float32 [16, 32], P('dp'), may hold values from -0.5 to 0.5
- rstd_one: float32 [16, 32], P('dp'), may hold values from 0.5 to 2
- gain_one: float32 [320], replicated, may hold values from 0.25 to 1.75
- shift_one: float32 [320], replicated, may hold values from -0.5 to 0.5
- kernel_one: bfloat16 [4, 9, 25600], P(None, None, 'dp'), may hold values from -0.109375 to 0.109375
- bias_one: float32 [320], replicated, may hold values from -3 to 3
- embed_bias: float32 [16, 320], P('dp'), may hold values from -3 to 3
- mean_two: float32 [16, 32], P('dp'), may hold values from -0.5 to 0.5
- rstd_two: float32 [16, 32], P('dp'), may hold values from 0.5 to 2
- gain_two: float32 [320], replicated, may hold values from 0.25 to 1.75
- shift_two: float32 [320], replicated, may hold values from -0.5 to 0.5
- kernel_two: bfloat16 [4, 9, 25600], P(None, None, 'dp'), may hold values from -0.109375 to 0.109375
- bias_two: float32 [320], replicated, may hold values from -3 to 3
Outputs:
- block_out: bfloat16 [16, 4, 128, 320], P('dp', 'rows')
All inputs are finite; a program needn't handle non-finite values.
Results may differ from a plain program's by a relative error of at most 0.0045.
Values may be sent and summed in bfloat16 or wider, within the bound.
No kernel may reach another device: no remote copies, remote signals or barrier semaphores. Data moves between devices by JAX's collectives and lax.ppermute only.
A program may use at most 192 MiB of HBM per device.

v0:
```python
import jax
import jax.numpy as jnp
from jax import lax
from jax.sharding import PartitionSpec as P


def padded_2(array, sides, width):
    for axis, dim in sides:
        devices, length = (lax.axis_size(axis), array.shape[dim])
        up = [(i, (i + 1) % devices) for i in range(devices - 1)]
        down = [(j, i) for i, j in up]
        last = lax.slice_in_dim(array, length - width, length, axis=dim)
        first = lax.slice_in_dim(array, 0, width, axis=dim)
        before = lax.ppermute(last, axis, up)
        after = lax.ppermute(first, axis, down)
        array = jnp.concatenate([before, array, after], axis=dim)
    return array


def norm_silu(values, group_mean, group_rstd, gain_vec, shift_vec):
    height, columns, channels = values.shape
    groups = group_mean.shape[-1]
    grouped = values.reshape(height, columns, groups, channels // groups)
    scaled = (grouped - group_mean[0][:, None]) * group_rstd[0][:, None]
    return jax.nn.silu(scaled.reshape(height, columns, channels) * gain_vec + shift_vec)


def padded_rows(activation):
    padded = padded_2(activation, (("rows", 0),), 1)
    return jnp.pad(padded, ((0, 0), (1, 1), (0, 0)))


def window_at(padded, position, height, columns, first_channel, depth):
    tap_row = position // 3
    tap_col = position % 3
    window = padded[
        tap_row : tap_row + height,
        tap_col : tap_col + columns,
        first_channel : first_channel + depth,
    ]
    return window.reshape(height * columns, depth)


def reorder_whole(whole_kernel, channels):
    blocks = whole_kernel.shape[0]
    split = whole_kernel.reshape(blocks, 9, channels // blocks, channels)
    return jnp.transpose(split, (1, 0, 2, 3)).reshape(3, 3 * channels, channels)


def whole_weights(kernel, channels):
    whole_kernel = lax.all_gather(kernel, "dp", axis=2, tiled=True)
    return reorder_whole(whole_kernel, channels)


def convolve_whole(activation, weights):
    height, columns, channels = activation.shape
    padded = padded_rows(activation)
    accumulated = jnp.zeros((height * columns, channels), jnp.float32)
    for tap_row in range(3):
        windows = jnp.concatenate(
            [
                window_at(padded, 3 * tap_row + tap_col, height, columns, 0, channels)
                for tap_col in range(3)
            ],
            axis=1,
        )
        accumulated = accumulated + jnp.dot(
            windows, weights[tap_row], preferred_element_type=jnp.float32
        )
    return accumulated.reshape(height, columns, channels)


def shards(
    latents,
    mean_one,
    rstd_one,
    gain_one,
    shift_one,
    kernel_one,
    bias_one,
    embed_bias,
    mean_two,
    rstd_two,
    gain_two,
    shift_two,
    kernel_two,
    bias_two,
):
    channels = latents.shape[3]
    sample = latents[0].astype(jnp.float32)
    first_act = norm_silu(sample, mean_one, rstd_one, gain_one, shift_one).astype(jnp.bfloat16)
    hidden = (
        convolve_whole(first_act, whole_weights(kernel_one, channels)) + bias_one + embed_bias[0]
    )
    second_act = norm_silu(hidden, mean_two, rstd_two, gain_two, shift_two).astype(jnp.bfloat16)
    result = convolve_whole(second_act, whole_weights(kernel_two, channels)) + bias_two + sample
    return result.astype(jnp.bfloat16)[None]


def solution(mesh):
    placed = (
        P("dp", "rows", None, None),
        P("dp", None),
        P("dp", None),
        P(),
        P(),
        P(None, None, "dp"),
        P(),
        P("dp", None),
        P("dp", None),
        P("dp", None),
        P(),
        P(),
        P(None, None, "dp"),
        P(),
    )
    return jax.shard_map(
        shards, mesh=mesh, in_specs=placed, out_specs=P("dp", "rows", None, None), check_vma=False
    )
```

profile of v0, /device:TPU:0, one launch (start us, length us, event | category | flops | bytes accessed | tf_op | source)
XLA Modules:
  0.0 321.2 jit_solution(16401829512371649083)
XLA Ops:
  6.5 3.1 copy.65
  9.7 0.0 all-gather.3.cloned.1.call-update
  9.7 0.0 copy-start.12
  9.7 0.0 copy-start
  9.7 0.0 all-gather.5.cloned.1.call-start
  9.8 2.4 copy.77
  12.2 0.0 all-gather.5.cloned.1.call-update
  12.2 0.0 copy-start.10
  12.2 0.1 mul.80
  12.3 0.1 mul.81
  12.4 0.1 sub.41
  12.5 0.1 sub.42
  12.6 0.3 multiply_convert_fusion.3
  12.9 4.9 %collective-permute-start = (bf16[1,128,320]{1,2,0:T(8,128)(2,1)S(1)}, bf16[1,128,320]{1,2,0:T(8,128)(2,1)S(1)}, u32[]{:S(2)}, u32[]{:S(2)}) collective-permute-start(bf16[1,128,320]{1,2,0:T(8,128)(2,1)S(1)} %get-tuple-element.29), channel_id=1, source_target_pairs={{0,1},{2,3},{4,5},{6,7},{8,9},{10,11},{12,13},{14,15},{16,17},{18,... | collective-permute-start | bytes 245768 | tf_op jit(solution)/shard_map/ppermute | solution.py:14
  17.8 1.3 collective-permute-start.1
  19.1 0.2 copy.68
  19.3 0.9 multiply_convert_fusion.2
  20.2 0.1 mul.93
  20.3 0.1 mul.94
  20.4 0.1 sub.48
  20.4 0.1 sub.49
  20.6 3.5 %collective-permute-done.1 = bf16[1,128,320]{1,2,0:T(8,128)(2,1)S(1)} collective-permute-done((bf16[1,128,320]{1,2,0:T(8,128)(2,1)S(1)}, bf16[1,128,320]{1,2,0:T(8,128)(2,1)S(1)}, u32[]{:S(2)}, u32[]{:S(2)}) %collective-permute-start.1) | collective-permute-done | bytes 81952 | tf_op jit(solution)/shard_map/ppermute | solution.py:15
  24.2 0.3 fusion.5
  24.5 0.2 slice_bitcast_fusion.7
  24.8 0.7 copy_bitcast_fusion.11
  25.5 120.5 %all-gather.3.cloned.1.call-done = bf16[4,9,25600]{1,0,2:T(4,128)(2,1)} async-done(((bf16[4,9,1600]{1,0,2:T(4,128)(2,1)}), bf16[4,9,25600]{1,0,2:T(4,128)(2,1)}) %all-gather.3.cloned.1.call-update) | async-done | bytes 1843216 | tf_op jit(solution)/shard_map/all_gather | solution.py:51
  146.0 30.0 %copy.66 = bf16[4,9,80,320]{3,2,0,1:T(8,128)(2,1)S(1)} copy(bf16[4,9,80,320]{1,0,3,2:T(4,128)(2,1)} %bitcast.136) | data formatting | bytes 3686400 | tf_op jit(solution)/shard_map/reshape | solution.py:46
  176.1 0.2 fusion.62
  176.3 0.0 copy-start.1
  176.3 0.4 fusion.6
  176.8 0.4 copy-done.1
  177.2 0.1 copy-done.2
  177.3 0.4 convolution_add_fusion.3
  177.8 0.6 multiply_convert_fusion
  178.4 0.3 multiply_convert_fusion.1
  178.8 3.4 %collective-permute-start.2 = (bf16[1,128,320]{1,2,0:T(8,128)(2,1)S(1)}, bf16[1,128,320]{1,2,0:T(8,128)(2,1)S(1)}, u32[]{:S(2)}, u32[]{:S(2)}) collective-permute-start(bf16[1,128,320]{1,2,0:T(8,128)(2,1)S(1)} %get-tuple-element.25), channel_id=1, source_target_pairs={{0,1},{2,3},{4,5},{6,7},{8,9},{10,11},{12,13},{14,15},{16,17},{18,... | collective-permute-start | bytes 245768 | tf_op jit(solution)/shard_map/ppermute | solution.py:14
  182.2 1.3 collective-permute-start.3
  183.5 97.6 %all-gather.5.cloned.1.call-done = bf16[4,9,25600]{1,0,2:T(4,128)(2,1)} async-done(((bf16[4,9,1600]{1,0,2:T(4,128)(2,1)}), bf16[4,9,25600]{1,0,2:T(4,128)(2,1)}) %all-gather.5.cloned.1.call-update) | async-done | bytes 1843216 | tf_op jit(solution)/shard_map/all_gather | solution.py:51
  281.1 29.7 %copy.78 = bf16[4,9,80,320]{3,2,0,1:T(8,128)(2,1)S(1)} copy(bf16[4,9,80,320]{1,0,3,2:T(4,128)(2,1)} %bitcast.135) | data formatting | bytes 3686400 | tf_op jit(solution)/shard_map/reshape | solution.py:46
  310.8 0.2 fusion.61
  311.2 0.3 select_maximum_fusion
  311.5 0.2 slice_bitcast_fusion.1
  312.0 0.4 fusion.22
  312.4 0.4 convolution_add_fusion.1
  312.9 0.4 convolution_add_fusion
  313.3 0.2 reshape.141
  313.5 0.1 copy-done.9
  313.5 0.8 fusion.50
  (43 shorter events, 0.5 us)
Async XLA Ops:
  6.5 3.3 %copy-start.3 = (bf16[4,9,1600]{2,0,1:T(4,128)(2,1)S(1)}, bf16[4,9,1600]{2,0,1:T(4,128)(2,1)}, u32[]{:S(2)}) copy-start(bf16[4,9,1600]{2,0,1:T(4,128)(2,1)} %param.26) | copy-start | bytes 345604
  6.5 139.5 %all-gather.3.cloned.1.call-start = ((), (), s32[]{:S(2)}) async-start(), calls=%async_computation | async-start | bytes 27852800 | tf_op jit(solution)/shard_map/all_gather | solution.py:51
  9.7 2.5 copy-start.11
  9.7 2.7 copy-start.12
  9.7 2.9 copy-start
  9.7 2.9 copy-start.4
  9.7 2.9 copy-start.5
  9.7 271.4 %all-gather.5.cloned.1.call-start = ((), (), s32[]{:S(2)}) async-start(), calls=%async_computation.1 | async-start | bytes 27852800 | tf_op jit(solution)/shard_map/all_gather | solution.py:51
  12.2 8.0 %copy-start.13 = (f32[1,32]{1,0:T(1,128)S(1)}, f32[1,32]{1,0:T(1,128)}, u32[]{:S(2)}) copy-start(f32[1,32]{1,0:T(1,128)} %param.23) | copy-start | bytes 388
  12.2 8.2 %copy-start.14 = (f32[1,32]{1,0:T(1,128)S(1)}, f32[1,32]{1,0:T(1,128)}, u32[]{:S(2)}) copy-start(f32[1,32]{1,0:T(1,128)} %param.22) | copy-start | bytes 388
  12.2 8.4 %copy-start.10 = (f32[1,320]{1,0:T(1,128)S(1)}, f32[1,320]{1,0:T(1,128)}, u32[]{:S(2)}) copy-start(f32[1,320]{1,0:T(1,128)} %param.21) | copy-start | bytes 3844
  12.9 7.7 %collective-permute-start = (bf16[1,128,320]{1,2,0:T(8,128)(2,1)S(1)}, bf16[1,128,320]{1,2,0:T(8,128)(2,1)S(1)}, u32[]{:S(2)}, u32[]{:S(2)}) collective-permute-start(bf16[1,128,320]{1,2,0:T(8,128)(2,1)S(1)} %get-tuple-element.29), channel_id=1, source_target_pairs={{0,1},{2,3},{4,5},{6,7},{8,9},{10,11},{12,13},{14,15},{16,17},{18,... | collective-permute-start | bytes 245768 | tf_op jit(solution)/shard_map/ppermute | solution.py:14
  17.8 6.3 %collective-permute-start.1 = (bf16[1,128,320]{1,2,0:T(8,128)(2,1)S(1)}, bf16[1,128,320]{1,2,0:T(8,128)(2,1)S(1)}, u32[]{:S(2)}, u32[]{:S(2)}) collective-permute-start(bf16[1,128,320]{1,2,0:T(8,128)(2,1)S(1)} %get-tuple-element.30), channel_id=1, source_target_pairs={{1,0},{3,2},{5,4},{7,6},{9,8},{11,10},{13,12},{15,14},{17,16},{19,... | collective-permute-start | bytes 245768 | tf_op jit(solution)/shard_map/ppermute | solution.py:15
  176.3 0.9 copy-start.1
  176.3 1.0 copy-start.2
  176.8 1.0 copy-start.6
  176.8 1.0 copy-start.7
  176.8 1.0 copy-start.8
  178.8 132.3 %collective-permute-start.2 = (bf16[1,128,320]{1,2,0:T(8,128)(2,1)S(1)}, bf16[1,128,320]{1,2,0:T(8,128)(2,1)S(1)}, u32[]{:S(2)}, u32[]{:S(2)}) collective-permute-start(bf16[1,128,320]{1,2,0:T(8,128)(2,1)S(1)} %get-tuple-element.25), channel_id=1, source_target_pairs={{0,1},{2,3},{4,5},{6,7},{8,9},{10,11},{12,13},{14,15},{16,17},{18,... | collective-permute-start | bytes 245768 | tf_op jit(solution)/shard_map/ppermute | solution.py:14
  182.2 128.9 %collective-permute-start.3 = (bf16[1,128,320]{1,2,0:T(8,128)(2,1)S(1)}, bf16[1,128,320]{1,2,0:T(8,128)(2,1)S(1)}, u32[]{:S(2)}, u32[]{:S(2)}) collective-permute-start(bf16[1,128,320]{1,2,0:T(8,128)(2,1)S(1)} %get-tuple-element.26), channel_id=1, source_target_pairs={{1,0},{3,2},{5,4},{7,6},{9,8},{11,10},{13,12},{15,14},{17,16},{19,... | collective-permute-start | bytes 245768 | tf_op jit(solution)/shard_map/ppermute | solution.py:15
  312.9 0.7 copy-start.9
Sparse Core Ops, SparseCore 0:
  9.8 136.1 all-gather.2
  147.6 133.4 all-gather.4
where the time goes:
time: 323 us; the launch traced here: 321 us
  waiting for transfers between devices  222 us (69%)
  local copies, waits for them, and re-layouts  68.9 us (21%)
  between operations  13.9 us (4%)
  starting transfers between devices  10.9 us (3%)
    all_gather x2, waiting for transfers between devices, whole_weights(): whole_kernel = lax.all_gather(kernel, 'dp', axis=2, tiled=True)  218 us
    reshape x2, local copies, waits for them, and re-layouts, reorder_whole(): split = whole_kernel.reshape(blocks, 9, channels // blocks, channels)  59.7 us
    ppermute x2, starting transfers between devices, padded_2(): before = lax.ppermute(last, axis, up)  8.29 us
    unnamed x34, local copies, waits for them, and re-layouts  6.57 us
  transfers between devices with their start and end apart: 6, of which 3 were waited for; matrix products, arithmetic and copies ran while one was open for 21% of the time, Pallas kernels for 0%

commit v1 on v0

--- a/solution.py
+++ b/solution.py
@@ -2,6 +2,12 @@
 import jax.numpy as jnp
 from jax import lax
 from jax.sharding import PartitionSpec as P
+
+
+def joined_along(tiles, dim):
+    tiles = jnp.moveaxis(tiles, 0, dim)
+    dims = tiles.shape
+    return tiles.reshape(*dims[:dim], dims[dim] * dims[dim + 1], *dims[dim + 2 :])
 
 
 def padded_2(array, sides, width):
@@ -48,7 +54,14 @@
 
 
 def whole_weights(kernel, channels):
-    whole_kernel = lax.all_gather(kernel, "dp", axis=2, tiled=True)
+    size = lax.axis_size("dp")
+    right = [(i_2, (i_2 + 1) % size) for i_2 in range(size)]
+    blocks_2 = [kernel]
+    while len(blocks_2) < size:
+        blocks_2.append(lax.ppermute(blocks_2[-1], "dp", right))
+    here = lax.axis_index("dp")
+    blocks_2 = jnp.stack(blocks_2)[(here - jnp.arange(size)) % size]
+    whole_kernel = joined_along(blocks_2, 2)
     return reorder_whole(whole_kernel, channels)
 
 

time: 323 us -> 150 us (0.46)
  waiting for transfers between devices: 222 us -> 75.7 us
  local copies, waits for them, and re-layouts: 68.9 us -> 50.3 us
  between operations: 13.9 us -> 0.56 us
  starting transfers between devices: 10.9 us -> 15.2 us
    all_gather x2 -> x0, waiting for transfers between devices: 218 us -> none  [whole_weights(): whole_kernel = lax.all_gather(kernel, 'dp', axis=2, tiled=True)]
    ppermute x0 -> x30, waiting for transfers between devices: none -> 75.6 us  [whole_weights(): blocks_2.append(lax.ppermute(blocks_2[-1], 'dp', right))]
    reshape x2 -> x0, local copies, waits for them, and re-layouts: 59.7 us -> none  [reorder_whole(): split = whole_kernel.reshape(blocks, 9, channels // blocks, channels)]
    unnamed x34 -> x50, local copies, waits for them, and re-layouts: 6.57 us -> 24.5 us
    another operation x0 -> x4, local copies, waits for them, and re-layouts: none -> 10.6 us  [the longest x2 8.31 us: reorder_whole(): split = whole_kernel.reshape(blocks, 9, channels // blocks, channels)]
    gather x0 -> x2, local copies, waits for them, and re-layouts: none -> 7.6 us  [whole_weights(): blocks_2 = jnp.stack(blocks_2)[(here - jnp.arange(size)) % size]]
    ppermute x0 -> x30, starting transfers between devices: none -> 3.69 us  [whole_weights(): blocks_2.append(lax.ppermute(blocks_2[-1], 'dp', right))]
    ppermute x2, waiting for transfers between devices: 3.53 us -> 0.01 us  [padded_2(): after = lax.ppermute(first, axis, down)]
  transfers between devices with their start and end apart: 6 -> 34, of which waited for: 3 -> 27; matrix products, arithmetic and copies ran while one was open for 21% -> 36% of each run, Pallas kernels for 0% -> 0%
where the time goes in v1:
time: 150 us; the launch traced here: 149 us
  waiting for transfers between devices  75.7 us (50%)
  local copies, waits for them, and re-layouts  50.3 us (34%)
  starting transfers between devices  15.2 us (10%)
  other arithmetic  4.64 us (3%)
  matrix products  2.73 us (2%)
    ppermute x30, waiting for transfers between devices, whole_weights(): blocks_2.append(lax.ppermute(blocks_2[-1], 'dp', right))  75.6 us
    unnamed x50, local copies, waits for them, and re-layouts  24.5 us
    ppermute x2, starting transfers between devices, padded_2(): before = lax.ppermute(last, axis, up)  8.67 us
    another operation x2, local copies, waits for them, and re-layouts, reorder_whole(): split = whole_kernel.reshape(blocks, 9, channels // blocks, channels)  8.31 us
    gather x2, local copies, waits for them, and re-layouts, whole_weights(): blocks_2 = jnp.stack(blocks_2)[(here - jnp.arange(size)) % size]  7.6 us
    ppermute x30, starting transfers between devices, whole_weights(): blocks_2.append(lax.ppermute(blocks_2[-1], 'dp', right))  3.69 us
  transfers between devices with their start and end apart: 34, of which 27 were waited for; matrix products, arithmetic and copies ran while one was open for 36% of the time, Pallas kernels for 0%

profile of v1, /device:TPU:0, one launch (start us, length us, event | category | flops | bytes accessed | tf_op | source)
XLA Modules:
  0.0 149.0 jit_solution(6850089787137108227)
XLA Ops:
  0.6 0.7 mul.80
  1.4 0.7 sub.56
  2.2 1.2 multiply_convert_fusion.3
  3.4 4.4 %collective-permute-start = (bf16[1,128,320]{1,2,0:T(8,128)(2,1)S(1)}, bf16[1,128,320]{1,2,0:T(8,128)(2,1)S(1)}, u32[]{:S(2)}, u32[]{:S(2)}) collective-permute-start(bf16[1,128,320]{1,2,0:T(8,128)(2,1)S(1)} %get-tuple-element.29), channel_id=1, source_target_pairs={{0,1},{2,3},{4,5},{6,7},{8,9},{10,11},{12,13},{14,15},{16,17},{18,... | collective-permute-start | bytes 245768 | tf_op jit(solution)/shard_map/ppermute | solution.py:20
  7.9 1.3 collective-permute-start.1
  9.2 1.4 collective-permute-start.19
  10.5 1.6 %bitcast_dynamic-update-slice_fusion.31 = bf16[16,4,9,1600]{3,1,2,0:T(4,128)(2,1)} fusion(bf16[4,9,1600]{2,0,1:T(4,128)(2,1)} %param.19), kind=kLoop, calls=%fused_computation.136 | loop fusion | bytes 235008
  12.1 1.1 copy.28
  13.2 1.6 %bitcast_dynamic-update-slice_fusion.15 = bf16[16,4,9,1600]{3,1,2,0:T(4,128)(2,1)} fusion(bf16[4,9,1600]{2,0,1:T(4,128)(2,1)} %param.26), kind=kLoop, calls=%fused_computation.120 | loop fusion | bytes 235008
  14.8 1.6 %multiply_convert_fusion.2 = bf16[256,320]{0,1:T(8,128)(2,1)} fusion(f32[40,8,2,128]{3,2,1,0:T(2,128)S(1)} %bitcast.209, f32[320]{0:T(512)} %param.18, f32[320]{0:T(512)} %param.17, f32[320]{0:T(512)S(1)} %mul.81, f32[320]{0:T(512)S(1)} %sub.57), kind=kLoop, calls=%fused_computation.67 | loop fusion | flops 737280 | bytes 496640 | tf_op jit(solution)/shard_map/convert_element_type | solution.py:104
  18.0 0.7 bitcast_dynamic-update-slice_fusion.30
  18.7 1.3 collective-permute-start.20
  20.1 0.7 bitcast_dynamic-update-slice_fusion.14
  20.7 3.9 %collective-permute-done.3 = bf16[4,9,1600]{2,0,1:T(4,128)(2,1)S(1)} collective-permute-done((bf16[4,9,1600]{2,0,1:T(4,128)(2,1)S(1)}, bf16[4,9,1600]{2,0,1:T(4,128)(2,1)S(1)}, u32[]{:S(2)}, u32[]{:S(2)}) %collective-permute-start.3) | collective-permute-done | bytes 115232 | tf_op jit(solution)/shard_map/ppermute | solution.py:61
  24.7 0.7 bitcast_dynamic-update-slice_fusion.29
  26.7 5.0 %collective-permute-done.4 = bf16[4,9,1600]{2,0,1:T(4,128)(2,1)S(1)} collective-permute-done((bf16[4,9,1600]{2,0,1:T(4,128)(2,1)S(1)}, bf16[4,9,1600]{2,0,1:T(4,128)(2,1)S(1)}, u32[]{:S(2)}, u32[]{:S(2)}) %collective-permute-start.4) | collective-permute-done | bytes 115232 | tf_op jit(solution)/shard_map/ppermute | solution.py:61
  33.6 5.0 %collective-permute-done.5 = bf16[4,9,1600]{2,0,1:T(4,128)(2,1)S(1)} collective-permute-done((bf16[4,9,1600]{2,0,1:T(4,128)(2,1)S(1)}, bf16[4,9,1600]{2,0,1:T(4,128)(2,1)S(1)}, u32[]{:S(2)}, u32[]{:S(2)}) %collective-permute-start.5) | collective-permute-done | bytes 115232 | tf_op jit(solution)/shard_map/ppermute | solution.py:61
  39.9 0.7 bitcast_dynamic-update-slice_fusion.11
  40.6 5.0 %collective-permute-done.6 = bf16[4,9,1600]{2,0,1:T(4,128)(2,1)S(1)} collective-permute-done((bf16[4,9,1600]{2,0,1:T(4,128)(2,1)S(1)}, bf16[4,9,1600]{2,0,1:T(4,128)(2,1)S(1)}, u32[]{:S(2)}, u32[]{:S(2)}) %collective-permute-start.6) | collective-permute-done | bytes 115232 | tf_op jit(solution)/shard_map/ppermute | solution.py:61
  45.6 0.7 bitcast_dynamic-update-slice_fusion.26
  47.6 5.0 %collective-permute-done.7 = bf16[4,9,1600]{2,0,1:T(4,128)(2,1)S(1)} collective-permute-done((bf16[4,9,1600]{2,0,1:T(4,128)(2,1)S(1)}, bf16[4,9,1600]{2,0,1:T(4,128)(2,1)S(1)}, u32[]{:S(2)}, u32[]{:S(2)}) %collective-permute-start.7) | collective-permute-done | bytes 115232 | tf_op jit(solution)/shard_map/ppermute | solution.py:61
  53.9 0.7 bitcast_dynamic-update-slice_fusion.9
  54.5 5.0 %collective-permute-done.8 = bf16[4,9,1600]{2,0,1:T(4,128)(2,1)S(1)} collective-permute-done((bf16[4,9,1600]{2,0,1:T(4,128)(2,1)S(1)}, bf16[4,9,1600]{2,0,1:T(4,128)(2,1)S(1)}, u32[]{:S(2)}, u32[]{:S(2)}) %collective-permute-start.8) | collective-permute-done | bytes 115232 | tf_op jit(solution)/shard_map/ppermute | solution.py:61
  60.8 0.7 bitcast_dynamic-update-slice_fusion.8
  61.5 5.0 %collective-permute-done.9 = bf16[4,9,1600]{2,0,1:T(4,128)(2,1)S(1)} collective-permute-done((bf16[4,9,1600]{2,0,1:T(4,128)(2,1)S(1)}, bf16[4,9,1600]{2,0,1:T(4,128)(2,1)S(1)}, u32[]{:S(2)}, u32[]{:S(2)}) %collective-permute-start.9) | collective-permute-done | bytes 115232 | tf_op jit(solution)/shard_map/ppermute | solution.py:61
  66.5 0.7 bitcast_dynamic-update-slice_fusion.23
  68.5 5.0 %collective-permute-done.10 = bf16[4,9,1600]{2,0,1:T(4,128)(2,1)S(1)} collective-permute-done((bf16[4,9,1600]{2,0,1:T(4,128)(2,1)S(1)}, bf16[4,9,1600]{2,0,1:T(4,128)(2,1)S(1)}, u32[]{:S(2)}, u32[]{:S(2)}) %collective-permute-start.10) | collective-permute-done | bytes 115232 | tf_op jit(solution)/shard_map/ppermute | solution.py:61
  74.8 0.7 bitcast_dynamic-update-slice_fusion.6
  75.5 5.0 %collective-permute-done.11 = bf16[4,9,1600]{2,0,1:T(4,128)(2,1)S(1)} collective-permute-done((bf16[4,9,1600]{2,0,1:T(4,128)(2,1)S(1)}, bf16[4,9,1600]{2,0,1:T(4,128)(2,1)S(1)}, u32[]{:S(2)}, u32[]{:S(2)}) %collective-permute-start.11) | collective-permute-done | bytes 115232 | tf_op jit(solution)/shard_map/ppermute | solution.py:61
  80.4 0.7 bitcast_dynamic-update-slice_fusion.21
  82.4 5.0 %collective-permute-done.12 = bf16[4,9,1600]{2,0,1:T(4,128)(2,1)S(1)} collective-permute-done((bf16[4,9,1600]{2,0,1:T(4,128)(2,1)S(1)}, bf16[4,9,1600]{2,0,1:T(4,128)(2,1)S(1)}, u32[]{:S(2)}, u32[]{:S(2)}) %collective-permute-start.12) | collective-permute-done | bytes 115232 | tf_op jit(solution)/shard_map/ppermute | solution.py:61
  87.4 0.7 bitcast_dynamic-update-slice_fusion.20
  89.4 5.0 %collective-permute-done.13 = bf16[4,9,1600]{2,0,1:T(4,128)(2,1)S(1)} collective-permute-done((bf16[4,9,1600]{2,0,1:T(4,128)(2,1)S(1)}, bf16[4,9,1600]{2,0,1:T(4,128)(2,1)S(1)}, u32[]{:S(2)}, u32[]{:S(2)}) %collective-permute-start.13) | collective-permute-done | bytes 115232 | tf_op jit(solution)/shard_map/ppermute | solution.py:61
  96.4 5.0 %collective-permute-done.14 = bf16[4,9,1600]{2,0,1:T(4,128)(2,1)S(1)} collective-permute-done((bf16[4,9,1600]{2,0,1:T(4,128)(2,1)S(1)}, bf16[4,9,1600]{2,0,1:T(4,128)(2,1)S(1)}, u32[]{:S(2)}, u32[]{:S(2)}) %collective-permute-start.14) | collective-permute-done | bytes 115232 | tf_op jit(solution)/shard_map/ppermute | solution.py:61
  103.3 5.0 %collective-permute-done.15 = bf16[4,9,1600]{2,0,1:T(4,128)(2,1)S(1)} collective-permute-done((bf16[4,9,1600]{2,0,1:T(4,128)(2,1)S(1)}, bf16[4,9,1600]{2,0,1:T(4,128)(2,1)S(1)}, u32[]{:S(2)}, u32[]{:S(2)}) %collective-permute-start.15) | collective-permute-done | bytes 115232 | tf_op jit(solution)/shard_map/ppermute | solution.py:61
  109.0 0.7 collective-permute-done.32
  109.7 1.6 %bitcast_dynamic-update-slice_fusion.1 = bf16[16,4,9,1600]{3,1,2,0:T(4,128)(2,1)} fusion(bf16[16,4,9,1600]{3,1,2,0:T(4,128)(2,1)} %bitcast_dynamic-update-slice_fusion.2, bf16[4,9,1600]{2,0,1:T(4,128)(2,1)} %collective-permute-done.32), kind=kLoop, calls=%fused_computation.106 | loop fusion | bytes 239616
  111.3 4.0 %collective-permute-done.16 = bf16[4,9,1600]{2,0,1:T(4,128)(2,1)S(1)} collective-permute-done((bf16[4,9,1600]{2,0,1:T(4,128)(2,1)S(1)}, bf16[4,9,1600]{2,0,1:T(4,128)(2,1)S(1)}, u32[]{:S(2)}, u32[]{:S(2)}) %collective-permute-start.16) | collective-permute-done | bytes 115232 | tf_op jit(solution)/shard_map/ppermute | solution.py:61
  116.0 3.8 %gather_fusion = bf16[16,4,9,1600]{3,1,2,0:T(4,128)(2,1)S(1)} fusion(bf16[16,4,9,1600]{3,1,2,0:T(4,128)(2,1)} %bitcast_dynamic-update-slice_fusion.16, s32[1024]{0:T(1024)S(1)} %pad_clamp_fusion), kind=kCustom, calls=%fused_computation | custom fusion | bytes 3686464 | tf_op jit(solution)/shard_map/gather | solution.py:63
  119.8 1.5 copy.25
  121.3 4.2 %reshape_reshape.6 = bf16[4,9,80,320]{3,2,1,0:T(8,128)(2,1)S(1)} reshape(bf16[4,9,16,1600]{3,2,1,0:T(8,128)(2,1)} %copy.25) | data formatting | bytes 3686400 | tf_op jit(solution)/shard_map/reshape;reshape | solution.py:52
  128.2 4.3 %collective-permute-start.17 = (bf16[1,128,320]{1,2,0:T(8,128)(2,1)S(1)}, bf16[1,128,320]{1,2,0:T(8,128)(2,1)S(1)}, u32[]{:S(2)}, u32[]{:S(2)}) collective-permute-start(bf16[1,128,320]{1,2,0:T(8,128)(2,1)S(1)} %get-tuple-element.25), channel_id=1, source_target_pairs={{0,1},{2,3},{4,5},{6,7},{8,9},{10,11},{12,13},{14,15},{16,17},{18,... | collective-permute-start | bytes 245768 | tf_op jit(solution)/shard_map/ppermute | solution.py:20
  132.4 1.5 %collective-permute-start.18 = (bf16[1,128,320]{1,2,0:T(8,128)(2,1)S(1)}, bf16[1,128,320]{1,2,0:T(8,128)(2,1)S(1)}, u32[]{:S(2)}, u32[]{:S(2)}) collective-permute-start(bf16[1,128,320]{1,2,0:T(8,128)(2,1)S(1)} %get-tuple-element.26), channel_id=1, source_target_pairs={{1,0},{3,2},{5,4},{7,6},{9,8},{11,10},{13,12},{15,14},{17,16},{19,... | collective-permute-start | bytes 245768 | tf_op jit(solution)/shard_map/ppermute | solution.py:21
  134.0 1.6 %bitcast_dynamic-update-slice_fusion = bf16[16,4,9,1600]{3,1,2,0:T(4,128)(2,1)} fusion(bf16[16,4,9,1600]{3,1,2,0:T(4,128)(2,1)} %bitcast_dynamic-update-slice_fusion.1, bf16[4,9,1600]{2,0,1:T(4,128)(2,1)} %collective-permute-done.33), kind=kLoop, calls=%fused_computation.105 | loop fusion | bytes 239616 | tf_op jit(solution)/shard_map/stack | solution.py:63
  135.6 3.8 %gather_fusion.1 = bf16[16,4,9,1600]{3,1,2,0:T(4,128)(2,1)S(1)} fusion(bf16[16,4,9,1600]{3,1,2,0:T(4,128)(2,1)} %bitcast_dynamic-update-slice_fusion, s32[1024]{0:T(1024)S(1)} %pad_clamp_fusion), kind=kCustom, calls=%fused_computation.1 | custom fusion | bytes 3686464 | tf_op jit(solution)/shard_map/gather | solution.py:63
  139.4 1.5 %copy.39 = bf16[4,9,16,1600]{3,2,1,0:T(8,128)(2,1)} copy(bf16[4,9,16,1600]{3,0,1,2:T(4,128)(2,1)S(1)} %bitcast.205) | data formatting | bytes 3686400 | tf_op jit(solution)/shard_map/transpose | solution.py:8
  140.9 4.2 %reshape_reshape.7 = bf16[4,9,80,320]{3,2,1,0:T(8,128)(2,1)S(1)} reshape(bf16[4,9,16,1600]{3,2,1,0:T(8,128)(2,1)} %copy.39) | data formatting | bytes 3686400 | tf_op jit(solution)/shard_map/reshape;reshape | solution.py:52
  148.2 0.8 fusion.50
  (127 shorter events, 26.7 us)
Async XLA Ops:
  0.0 16.5 %copy-start.7 = (f32[1,32]{1,0:T(1,128)S(1)}, f32[1,32]{1,0:T(1,128)}, u32[]{:S(2)}) copy-start(f32[1,32]{1,0:T(1,128)} %param.23) | copy-start | bytes 388
  0.0 16.6 %copy-start.8 = (f32[1,32]{1,0:T(1,128)S(1)}, f32[1,32]{1,0:T(1,128)}, u32[]{:S(2)}) copy-start(f32[1,32]{1,0:T(1,128)} %param.22) | copy-start | bytes 388
  0.0 16.8 %copy-start.6 = (f32[1,320]{1,0:T(1,128)S(1)}, f32[1,320]{1,0:T(1,128)}, u32[]{:S(2)}) copy-start(f32[1,320]{1,0:T(1,128)} %param.21) | copy-start | bytes 3844
  0.0 17.6 %collective-permute-start.2 = (bf16[4,9,1600]{2,0,1:T(4,128)(2,1)}, bf16[4,9,1600]{2,0,1:T(4,128)(2,1)S(1)}, u32[]{:S(2)}, u32[]{:S(2)}) collective-permute-start(bf16[4,9,1600]{2,0,1:T(4,128)(2,1)} %param.19), channel_id=1, source_target_pairs={{0,2},{2,4},{4,6},{6,8},{8,10},{10,12},{12,14},{14,16},{16,18},{18... | collective-permute-start | bytes 345608 | tf_op jit(solution)/shard_map/ppermute | solution.py:61
  3.4 13.4 %collective-permute-start = (bf16[1,128,320]{1,2,0:T(8,128)(2,1)S(1)}, bf16[1,128,320]{1,2,0:T(8,128)(2,1)S(1)}, u32[]{:S(2)}, u32[]{:S(2)}) collective-permute-start(bf16[1,128,320]{1,2,0:T(8,128)(2,1)S(1)} %get-tuple-element.29), channel_id=1, source_target_pairs={{0,1},{2,3},{4,5},{6,7},{8,9},{10,11},{12,13},{14,15},{16,17},{18,... | collective-permute-start | bytes 245768 | tf_op jit(solution)/shard_map/ppermute | solution.py:20
  7.9 9.0 %collective-permute-start.1 = (bf16[1,128,320]{1,2,0:T(8,128)(2,1)S(1)}, bf16[1,128,320]{1,2,0:T(8,128)(2,1)S(1)}, u32[]{:S(2)}, u32[]{:S(2)}) collective-permute-start(bf16[1,128,320]{1,2,0:T(8,128)(2,1)S(1)} %get-tuple-element.30), channel_id=1, source_target_pairs={{1,0},{3,2},{5,4},{7,6},{9,8},{11,10},{13,12},{15,14},{17,16},{19,... | collective-permute-start | bytes 245768 | tf_op jit(solution)/shard_map/ppermute | solution.py:21
  9.2 9.6 %collective-permute-start.19 = (bf16[4,9,1600]{2,0,1:T(4,128)(2,1)}, bf16[4,9,1600]{2,0,1:T(4,128)(2,1)S(1)}, u32[]{:S(2)}, u32[]{:S(2)}) collective-permute-start(bf16[4,9,1600]{2,0,1:T(4,128)(2,1)} %param.26), channel_id=1, source_target_pairs={{0,2},{2,4},{4,6},{6,8},{8,10},{10,12},{12,14},{14,16},{16,18},{18... | collective-permute-start | bytes 345608 | tf_op jit(solution)/shard_map/ppermute | solution.py:61
  17.7 7.0 %collective-permute-start.3 = (bf16[4,9,1600]{2,0,1:T(4,128)(2,1)S(1)}, bf16[4,9,1600]{2,0,1:T(4,128)(2,1)S(1)}, u32[]{:S(2)}, u32[]{:S(2)}) collective-permute-start(bf16[4,9,1600]{2,0,1:T(4,128)(2,1)S(1)} %collective-permute-done.2), channel_id=1, source_target_pairs={{0,2},{2,4},{4,6},{6,8},{8,10},{10,12},{12,14},{14,16},{16,18},{18... | collective-permute-start | bytes 345608 | tf_op jit(solution)/shard_map/ppermute | solution.py:61
  18.7 7.3 %collective-permute-start.20 = (bf16[4,9,1600]{2,0,1:T(4,128)(2,1)S(1)}, bf16[4,9,1600]{2,0,1:T(4,128)(2,1)S(1)}, u32[]{:S(2)}, u32[]{:S(2)}) collective-permute-start(bf16[4,9,1600]{2,0,1:T(4,128)(2,1)S(1)} %collective-permute-done.19), channel_id=1, source_target_pairs={{0,2},{2,4},{4,6},{6,8},{8,10},{10,12},{12,14},{14,16},{16,18},{18... | collective-permute-start | bytes 345608 | tf_op jit(solution)/shard_map/ppermute | solution.py:61
  24.7 7.0 %collective-permute-start.4 = (bf16[4,9,1600]{2,0,1:T(4,128)(2,1)S(1)}, bf16[4,9,1600]{2,0,1:T(4,128)(2,1)S(1)}, u32[]{:S(2)}, u32[]{:S(2)}) collective-permute-start(bf16[4,9,1600]{2,0,1:T(4,128)(2,1)S(1)} %collective-permute-done.3), channel_id=1, source_target_pairs={{0,2},{2,4},{4,6},{6,8},{8,10},{10,12},{12,14},{14,16},{16,18},{18... | collective-permute-start | bytes 345608 | tf_op jit(solution)/shard_map/ppermute | solution.py:61
  26.0 7.0 %collective-permute-start.21 = (bf16[4,9,1600]{2,0,1:T(4,128)(2,1)S(1)}, bf16[4,9,1600]{2,0,1:T(4,128)(2,1)S(1)}, u32[]{:S(2)}, u32[]{:S(2)}) collective-permute-start(bf16[4,9,1600]{2,0,1:T(4,128)(2,1)S(1)} %collective-permute-done.20), channel_id=1, source_target_pairs={{0,2},{2,4},{4,6},{6,8},{8,10},{10,12},{12,14},{14,16},{16,18},{18... | collective-permute-start | bytes 345608 | tf_op jit(solution)/shard_map/ppermute | solution.py:61
  31.7 7.0 %collective-permute-start.5 = (bf16[4,9,1600]{2,0,1:T(4,128)(2,1)S(1)}, bf16[4,9,1600]{2,0,1:T(4,128)(2,1)S(1)}, u32[]{:S(2)}, u32[]{:S(2)}) collective-permute-start(bf16[4,9,1600]{2,0,1:T(4,128)(2,1)S(1)} %collective-permute-done.4), channel_id=1, source_target_pairs={{0,2},{2,4},{4,6},{6,8},{8,10},{10,12},{12,14},{14,16},{16,18},{18... | collective-permute-start | bytes 345608 | tf_op jit(solution)/shard_map/ppermute | solution.py:61
  32.9 7.0 %collective-permute-start.22 = (bf16[4,9,1600]{2,0,1:T(4,128)(2,1)S(1)}, bf16[4,9,1600]{2,0,1:T(4,128)(2,1)S(1)}, u32[]{:S(2)}, u32[]{:S(2)}) collective-permute-start(bf16[4,9,1600]{2,0,1:T(4,128)(2,1)S(1)} %collective-permute-done.21), channel_id=1, source_target_pairs={{0,2},{2,4},{4,6},{6,8},{8,10},{10,12},{12,14},{14,16},{16,18},{18... | collective-permute-start | bytes 345608 | tf_op jit(solution)/shard_map/ppermute | solution.py:61
  38.6 7.0 %collective-permute-start.6 = (bf16[4,9,1600]{2,0,1:T(4,128)(2,1)S(1)}, bf16[4,9,1600]{2,0,1:T(4,128)(2,1)S(1)}, u32[]{:S(2)}, u32[]{:S(2)}) collective-permute-start(bf16[4,9,1600]{2,0,1:T(4,128)(2,1)S(1)} %collective-permute-done.5), channel_id=1, source_target_pairs={{0,2},{2,4},{4,6},{6,8},{8,10},{10,12},{12,14},{14,16},{16,18},{18... | collective-permute-start | bytes 345608 | tf_op jit(solution)/shard_map/ppermute | solution.py:61
  39.9 7.0 %collective-permute-start.23 = (bf16[4,9,1600]{2,0,1:T(4,128)(2,1)S(1)}, bf16[4,9,1600]{2,0,1:T(4,128)(2,1)S(1)}, u32[]{:S(2)}, u32[]{:S(2)}) collective-permute-start(bf16[4,9,1600]{2,0,1:T(4,128)(2,1)S(1)} %collective-permute-done.22), channel_id=1, source_target_pairs={{0,2},{2,4},{4,6},{6,8},{8,10},{10,12},{12,14},{14,16},{16,18},{18... | collective-permute-start | bytes 345608 | tf_op jit(solution)/shard_map/ppermute | solution.py:61
  45.6 7.0 %collective-permute-start.7 = (bf16[4,9,1600]{2,0,1:T(4,128)(2,1)S(1)}, bf16[4,9,1600]{2,0,1:T(4,128)(2,1)S(1)}, u32[]{:S(2)}, u32[]{:S(2)}) collective-permute-start(bf16[4,9,1600]{2,0,1:T(4,128)(2,1)S(1)} %collective-permute-done.6), channel_id=1, source_target_pairs={{0,2},{2,4},{4,6},{6,8},{8,10},{10,12},{12,14},{14,16},{16,18},{18... | collective-permute-start | bytes 345608 | tf_op jit(solution)/shard_map/ppermute | solution.py:61
  46.9 7.0 %collective-permute-start.24 = (bf16[4,9,1600]{2,0,1:T(4,128)(2,1)S(1)}, bf16[4,9,1600]{2,0,1:T(4,128)(2,1)S(1)}, u32[]{:S(2)}, u32[]{:S(2)}) collective-permute-start(bf16[4,9,1600]{2,0,1:T(4,128)(2,1)S(1)} %collective-permute-done.23), channel_id=1, source_target_pairs={{0,2},{2,4},{4,6},{6,8},{8,10},{10,12},{12,14},{14,16},{16,18},{18... | collective-permute-start | bytes 345608 | tf_op jit(solution)/shard_map/ppermute | solution.py:61
  52.6 7.0 %collective-permute-start.8 = (bf16[4,9,1600]{2,0,1:T(4,128)(2,1)S(1)}, bf16[4,9,1600]{2,0,1:T(4,128)(2,1)S(1)}, u32[]{:S(2)}, u32[]{:S(2)}) collective-permute-start(bf16[4,9,1600]{2,0,1:T(4,128)(2,1)S(1)} %collective-permute-done.7), channel_id=1, source_target_pairs={{0,2},{2,4},{4,6},{6,8},{8,10},{10,12},{12,14},{14,16},{16,18},{18... | collective-permute-start | bytes 345608 | tf_op jit(solution)/shard_map/ppermute | solution.py:61
  53.9 7.0 %collective-permute-start.25 = (bf16[4,9,1600]{2,0,1:T(4,128)(2,1)S(1)}, bf16[4,9,1600]{2,0,1:T(4,128)(2,1)S(1)}, u32[]{:S(2)}, u32[]{:S(2)}) collective-permute-start(bf16[4,9,1600]{2,0,1:T(4,128)(2,1)S(1)} %collective-permute-done.24), channel_id=1, source_target_pairs={{0,2},{2,4},{4,6},{6,8},{8,10},{10,12},{12,14},{14,16},{16,18},{18... | collective-permute-start | bytes 345608 | tf_op jit(solution)/shard_map/ppermute | solution.py:61
  59.5 7.0 %collective-permute-start.9 = (bf16[4,9,1600]{2,0,1:T(4,128)(2,1)S(1)}, bf16[4,9,1600]{2,0,1:T(4,128)(2,1)S(1)}, u32[]{:S(2)}, u32[]{:S(2)}) collective-permute-start(bf16[4,9,1600]{2,0,1:T(4,128)(2,1)S(1)} %collective-permute-done.8), channel_id=1, source_target_pairs={{0,2},{2,4},{4,6},{6,8},{8,10},{10,12},{12,14},{14,16},{16,18},{18... | collective-permute-start | bytes 345608 | tf_op jit(solution)/shard_map/ppermute | solution.py:61
  60.8 7.0 %collective-permute-start.26 = (bf16[4,9,1600]{2,0,1:T(4,128)(2,1)S(1)}, bf16[4,9,1600]{2,0,1:T(4,128)(2,1)S(1)}, u32[]{:S(2)}, u32[]{:S(2)}) collective-permute-start(bf16[4,9,1600]{2,0,1:T(4,128)(2,1)S(1)} %collective-permute-done.25), channel_id=1, source_target_pairs={{0,2},{2,4},{4,6},{6,8},{8,10},{10,12},{12,14},{14,16},{16,18},{18... | collective-permute-start | bytes 345608 | tf_op jit(solution)/shard_map/ppermute | solution.py:61
  66.5 7.0 %collective-permute-start.10 = (bf16[4,9,1600]{2,0,1:T(4,128)(2,1)S(1)}, bf16[4,9,1600]{2,0,1:T(4,128)(2,1)S(1)}, u32[]{:S(2)}, u32[]{:S(2)}) collective-permute-start(bf16[4,9,1600]{2,0,1:T(4,128)(2,1)S(1)} %collective-permute-done.9), channel_id=1, source_target_pairs={{0,2},{2,4},{4,6},{6,8},{8,10},{10,12},{12,14},{14,16},{16,18},{18... | collective-permute-start | bytes 345608 | tf_op jit(solution)/shard_map/ppermute | solution.py:61
  67.8 7.0 %collective-permute-start.27 = (bf16[4,9,1600]{2,0,1:T(4,128)(2,1)S(1)}, bf16[4,9,1600]{2,0,1:T(4,128)(2,1)S(1)}, u32[]{:S(2)}, u32[]{:S(2)}) collective-permute-start(bf16[4,9,1600]{2,0,1:T(4,128)(2,1)S(1)} %collective-permute-done.26), channel_id=1, source_target_pairs={{0,2},{2,4},{4,6},{6,8},{8,10},{10,12},{12,14},{14,16},{16,18},{18... | collective-permute-start | bytes 345608 | tf_op jit(solution)/shard_map/ppermute | solution.py:61
  73.5 7.0 %collective-permute-start.11 = (bf16[4,9,1600]{2,0,1:T(4,128)(2,1)S(1)}, bf16[4,9,1600]{2,0,1:T(4,128)(2,1)S(1)}, u32[]{:S(2)}, u32[]{:S(2)}) collective-permute-start(bf16[4,9,1600]{2,0,1:T(4,128)(2,1)S(1)} %collective-permute-done.10), channel_id=1, source_target_pairs={{0,2},{2,4},{4,6},{6,8},{8,10},{10,12},{12,14},{14,16},{16,18},{18... | collective-permute-start | bytes 345608 | tf_op jit(solution)/shard_map/ppermute | solution.py:61
  74.8 7.0 %collective-permute-start.28 = (bf16[4,9,1600]{2,0,1:T(4,128)(2,1)S(1)}, bf16[4,9,1600]{2,0,1:T(4,128)(2,1)S(1)}, u32[]{:S(2)}, u32[]{:S(2)}) collective-permute-start(bf16[4,9,1600]{2,0,1:T(4,128)(2,1)S(1)} %collective-permute-done.27), channel_id=1, source_target_pairs={{0,2},{2,4},{4,6},{6,8},{8,10},{10,12},{12,14},{14,16},{16,18},{18... | collective-permute-start | bytes 345608 | tf_op jit(solution)/shard_map/ppermute | solution.py:61
  80.4 7.0 %collective-permute-start.12 = (bf16[4,9,1600]{2,0,1:T(4,128)(2,1)S(1)}, bf16[4,9,1600]{2,0,1:T(4,128)(2,1)S(1)}, u32[]{:S(2)}, u32[]{:S(2)}) collective-permute-start(bf16[4,9,1600]{2,0,1:T(4,128)(2,1)S(1)} %collective-permute-done.11), channel_id=1, source_target_pairs={{0,2},{2,4},{4,6},{6,8},{8,10},{10,12},{12,14},{14,16},{16,18},{18... | collective-permute-start | bytes 345608 | tf_op jit(solution)/shard_map/ppermute | solution.py:61
  81.7 7.0 %collective-permute-start.29 = (bf16[4,9,1600]{2,0,1:T(4,128)(2,1)S(1)}, bf16[4,9,1600]{2,0,1:T(4,128)(2,1)S(1)}, u32[]{:S(2)}, u32[]{:S(2)}) collective-permute-start(bf16[4,9,1600]{2,0,1:T(4,128)(2,1)S(1)} %collective-permute-done.28), channel_id=1, source_target_pairs={{0,2},{2,4},{4,6},{6,8},{8,10},{10,12},{12,14},{14,16},{16,18},{18... | collective-permute-start | bytes 345608 | tf_op jit(solution)/shard_map/ppermute | solution.py:61
  87.4 7.0 %collective-permute-start.13 = (bf16[4,9,1600]{2,0,1:T(4,128)(2,1)S(1)}, bf16[4,9,1600]{2,0,1:T(4,128)(2,1)S(1)}, u32[]{:S(2)}, u32[]{:S(2)}) collective-permute-start(bf16[4,9,1600]{2,0,1:T(4,128)(2,1)S(1)} %collective-permute-done.12), channel_id=1, source_target_pairs={{0,2},{2,4},{4,6},{6,8},{8,10},{10,12},{12,14},{14,16},{16,18},{18... | collective-permute-start | bytes 345608 | tf_op jit(solution)/shard_map/ppermute | solution.py:61
  88.7 7.0 %collective-permute-start.30 = (bf16[4,9,1600]{2,0,1:T(4,128)(2,1)S(1)}, bf16[4,9,1600]{2,0,1:T(4,128)(2,1)S(1)}, u32[]{:S(2)}, u32[]{:S(2)}) collective-permute-start(bf16[4,9,1600]{2,0,1:T(4,128)(2,1)S(1)} %collective-permute-done.29), channel_id=1, source_target_pairs={{0,2},{2,4},{4,6},{6,8},{8,10},{10,12},{12,14},{14,16},{16,18},{18... | collective-permute-start | bytes 345608 | tf_op jit(solution)/shard_map/ppermute | solution.py:61
  94.4 7.0 %collective-permute-start.14 = (bf16[4,9,1600]{2,0,1:T(4,128)(2,1)S(1)}, bf16[4,9,1600]{2,0,1:T(4,128)(2,1)S(1)}, u32[]{:S(2)}, u32[]{:S(2)}) collective-permute-start(bf16[4,9,1600]{2,0,1:T(4,128)(2,1)S(1)} %collective-permute-done.13), channel_id=1, source_target_pairs={{0,2},{2,4},{4,6},{6,8},{8,10},{10,12},{12,14},{14,16},{16,18},{18... | collective-permute-start | bytes 345608 | tf_op jit(solution)/shard_map/ppermute | solution.py:61
  95.7 7.0 %collective-permute-start.31 = (bf16[4,9,1600]{2,0,1:T(4,128)(2,1)S(1)}, bf16[4,9,1600]{2,0,1:T(4,128)(2,1)S(1)}, u32[]{:S(2)}, u32[]{:S(2)}) collective-permute-start(bf16[4,9,1600]{2,0,1:T(4,128)(2,1)S(1)} %collective-permute-done.30), channel_id=1, source_target_pairs={{0,2},{2,4},{4,6},{6,8},{8,10},{10,12},{12,14},{14,16},{16,18},{18... | collective-permute-start | bytes 345608 | tf_op jit(solution)/shard_map/ppermute | solution.py:61
  101.4 7.0 %collective-permute-start.15 = (bf16[4,9,1600]{2,0,1:T(4,128)(2,1)S(1)}, bf16[4,9,1600]{2,0,1:T(4,128)(2,1)S(1)}, u32[]{:S(2)}, u32[]{:S(2)}) collective-permute-start(bf16[4,9,1600]{2,0,1:T(4,128)(2,1)S(1)} %collective-permute-done.14), channel_id=1, source_target_pairs={{0,2},{2,4},{4,6},{6,8},{8,10},{10,12},{12,14},{14,16},{16,18},{18... | collective-permute-start | bytes 345608 | tf_op jit(solution)/shard_map/ppermute | solution.py:61
  102.6 7.1 %collective-permute-start.32 = (bf16[4,9,1600]{2,0,1:T(4,128)(2,1)S(1)}, bf16[4,9,1600]{2,0,1:T(4,128)(2,1)}, u32[]{:S(2)}, u32[]{:S(2)}) collective-permute-start(bf16[4,9,1600]{2,0,1:T(4,128)(2,1)S(1)} %collective-permute-done.31), channel_id=1, source_target_pairs={{0,2},{2,4},{4,6},{6,8},{8,10},{10,12},{12,14},{14,16},{16,18},{18... | collective-permute-start | bytes 345608 | tf_op jit(solution)/shard_map/ppermute | solution.py:61
  108.3 7.0 %collective-permute-start.16 = (bf16[4,9,1600]{2,0,1:T(4,128)(2,1)S(1)}, bf16[4,9,1600]{2,0,1:T(4,128)(2,1)S(1)}, u32[]{:S(2)}, u32[]{:S(2)}) collective-permute-start(bf16[4,9,1600]{2,0,1:T(4,128)(2,1)S(1)} %collective-permute-done.15), channel_id=1, source_target_pairs={{0,2},{2,4},{4,6},{6,8},{8,10},{10,12},{12,14},{14,16},{16,18},{18... | collective-permute-start | bytes 345608 | tf_op jit(solution)/shard_map/ppermute | solution.py:61
  109.7 24.3 %collective-permute-start.33 = (bf16[4,9,1600]{2,0,1:T(4,128)(2,1)}, bf16[4,9,1600]{2,0,1:T(4,128)(2,1)}, u32[]{:S(2)}, u32[]{:S(2)}) collective-permute-start(bf16[4,9,1600]{2,0,1:T(4,128)(2,1)} %collective-permute-done.32), channel_id=1, source_target_pairs={{0,2},{2,4},{4,6},{6,8},{8,10},{10,12},{12,14},{14,16},{16,18},{18... | collective-permute-start | bytes 345608 | tf_op jit(solution)/shard_map/ppermute | solution.py:61
  125.8 0.9 copy-start.1
  125.9 1.3 copy-start.2
  125.9 1.3 copy-start.3
  125.9 1.3 copy-start.4
  128.2 17.4 %collective-permute-start.17 = (bf16[1,128,320]{1,2,0:T(8,128)(2,1)S(1)}, bf16[1,128,320]{1,2,0:T(8,128)(2,1)S(1)}, u32[]{:S(2)}, u32[]{:S(2)}) collective-permute-start(bf16[1,128,320]{1,2,0:T(8,128)(2,1)S(1)} %get-tuple-element.25), channel_id=1, source_target_pairs={{0,1},{2,3},{4,5},{6,7},{8,9},{10,11},{12,13},{14,15},{16,17},{18,... | collective-permute-start | bytes 245768 | tf_op jit(solution)/shard_map/ppermute | solution.py:20
  132.4 13.1 %collective-permute-start.18 = (bf16[1,128,320]{1,2,0:T(8,128)(2,1)S(1)}, bf16[1,128,320]{1,2,0:T(8,128)(2,1)S(1)}, u32[]{:S(2)}, u32[]{:S(2)}) collective-permute-start(bf16[1,128,320]{1,2,0:T(8,128)(2,1)S(1)} %get-tuple-element.26), channel_id=1, source_target_pairs={{1,0},{3,2},{5,4},{7,6},{9,8},{11,10},{13,12},{15,14},{17,16},{19,... | collective-permute-start | bytes 245768 | tf_op jit(solution)/shard_map/ppermute | solution.py:21
  147.3 0.9 copy-start
  147.3 0.9 copy-start.5
